TPU v7x, 32 devices: a whole 2x2x4 slice. The times are simulated.
32 devices in a mesh: quad: 2 (over x), py: 4 (over y, core), pz: 4 (over z).
Axes of the slice: x: 2, y: 2, z: 4, core: 2. Of those that a mesh axis runs over, the one named last changes fastest.
Arguments:
- source_real: float32 [4, 16, 64, 512], P(None, None, 'py', 'pz'), may hold values from -6 to 6
- source_imag: float32 [4, 16, 64, 512], P(None, None, 'py', 'pz'), may hold values from -2 to 2
- potential: float32 [16, 64, 512], P(None, 'py', 'pz'), may hold values from 0 to 2
- center: float32 [1], replicated, may hold values from 4.5 to 6
- radius: float32 [1], replicated, may hold values from 1 to 2
Outputs:
- moments: float32 [4, 2, 4, 16, 64, 512], P(None, None, None, 'quad', 'py', 'pz')
All inputs are finite; a program needn't handle non-finite values.
Results may differ from a plain program's by a relative error of at most 0.0003.
Values sent between devices are 32-bit elements; how exact they have to be, the bound alone decides.
No kernel may reach another device: no remote copies, remote signals or barrier semaphores. Data moves between devices by JAX's collectives and lax.ppermute only.
A program may use at most 256 MiB of HBM per device.

v0:
```python
import math
import jax
import jax.numpy as jnp
from jax import lax
from jax.sharding import PartitionSpec as P

QPTS = 8
MOMS = 4
stencil_weights = (-205.0 / 72.0, 8.0 / 5.0, -1.0 / 5.0, 8.0 / 315.0, -1.0 / 560.0)


def padded_2(block, sides, width):
    for axis, dim in sides:
        count = lax.axis_size(axis)
        forward = [(i, i + 1) for i in range(count - 1)]
        forward.append((count - 1, 0))
        backward = [(target, source) for source, target in forward]
        low = lax.ppermute(
            lax.slice_in_dim(block, block.shape[dim] - width, None, axis=dim), axis, forward
        )
        high = lax.ppermute(lax.slice_in_dim(block, 0, width, axis=dim), axis, backward)
        block = jnp.concatenate([low, block, high], axis=dim)
    return block


def apply_operator(field, potential):
    padded = padded_2(field, (("py", 4), ("pz", 5)), 4)
    width_y = field.shape[4]
    width_z = field.shape[5]
    laplace = 3.0 * stencil_weights[0] * field
    for offset in range(1, 5):
        beside_all = jnp.roll(field, offset, 3) + jnp.roll(field, -offset, 3)
        beside_all = (
            beside_all + padded[:, :, :, :, 4 + offset : 4 + offset + width_y, 4 : 4 + width_z]
        )
        beside_all = (
            beside_all + padded[:, :, :, :, 4 - offset : 4 - offset + width_y, 4 : 4 + width_z]
        )
        beside_all = (
            beside_all + padded[:, :, :, :, 4 : 4 + width_y, 4 + offset : 4 + offset + width_z]
        )
        beside_all = (
            beside_all + padded[:, :, :, :, 4 : 4 + width_y, 4 - offset : 4 - offset + width_z]
        )
        laplace = laplace + stencil_weights[offset] * beside_all
    return -0.5 * laplace + potential * field


def complex_mul(left, right):
    return (left[0] * right[0] - left[1] * right[1], left[0] * right[1] + left[1] * right[0])


def complex_div(left, right):
    norm_sq = right[0] * right[0] + right[1] * right[1]
    return (
        (left[0] * right[0] + left[1] * right[1]) / norm_sq,
        (left[1] * right[0] - left[0] * right[1]) / norm_sq,
    )


def local_bilinear(left, right):
    both = complex_mul(left, right)
    return (jnp.sum(both[0], axis=(-3, -2, -1)), jnp.sum(both[1], axis=(-3, -2, -1)))


def spread(value):
    return (value[0][..., None, None, None], value[1][..., None, None, None])


def moment_terms(solution, angles, radius_value):
    orders = jnp.arange(1, MOMS + 1).astype(jnp.float32)
    phase = orders[:, None] * angles[None, :]
    weight_re = radius_value / QPTS * jnp.cos(phase)
    weight_im = radius_value / QPTS * jnp.sin(phase)
    highest = lax.Precision.HIGHEST
    real_part = jnp.einsum("kq,qsxyz->ksxyz", weight_re, solution[:, 0], precision=highest)
    real_part = real_part - jnp.einsum(
        "kq,qsxyz->ksxyz", weight_im, solution[:, 1], precision=highest
    )
    imag_part = jnp.einsum("kq,qsxyz->ksxyz", weight_re, solution[:, 1], precision=highest)
    imag_part = imag_part + jnp.einsum(
        "kq,qsxyz->ksxyz", weight_im, solution[:, 0], precision=highest
    )
    return jnp.stack([real_part, imag_part], 1)


def per_device(source_real, source_imag, potential, center, radius):
    groups = lax.axis_size("quad")
    local_count = QPTS // groups
    first_point = lax.axis_index("quad") * local_count
    indices = (first_point + jnp.arange(local_count)).astype(jnp.float32)
    angles = 2.0 * math.pi * (indices + 0.5) / QPTS
    shift_re = center[0] + radius[0] * jnp.cos(angles)
    shift_im = radius[0] * jnp.sin(angles)
    shift_pair = (shift_re[:, None], shift_im[:, None])
    shift_field = (shift_re[:, None, None, None, None], shift_im[:, None, None, None, None])
    source = (source_real, source_imag)
    applied = apply_operator(jnp.stack(source)[None], potential)[0]
    hsource = (applied[0], applied[1])
    rho_local = local_bilinear(source, source)
    curv_local = local_bilinear(source, hsource)
    totals = lax.psum((rho_local[0], rho_local[1], curv_local[0], curv_local[1]), ("py", "pz"))
    rho_first = (totals[0], totals[1])
    curv_first = (totals[2], totals[3])
    scaled = complex_mul(shift_pair, rho_first)
    denom = (scaled[0] - curv_first[0], scaled[1] - curv_first[1])
    alpha_first = complex_div(rho_first, denom)
    alpha_wide = spread(alpha_first)
    first_iterate = complex_mul(alpha_wide, source)
    shifted = complex_mul(shift_field, source)
    image = (shifted[0] - hsource[0], shifted[1] - hsource[1])
    moved = complex_mul(alpha_wide, image)
    residual = (source[0] - moved[0], source[1] - moved[1])
    hres = apply_operator(jnp.stack(residual, 1), potential)
    shifted_res = complex_mul(shift_field, residual)
    image_res = (shifted_res[0] - hres[:, 0], shifted_res[1] - hres[:, 1])
    rho_part = local_bilinear(residual, residual)
    mixed_part = local_bilinear(residual, image_res)
    paired = lax.psum((rho_part[0], rho_part[1], mixed_part[0], mixed_part[1]), ("py", "pz"))
    rho_next = (paired[0], paired[1])
    mixed = (paired[2], paired[3])
    beta = complex_div(rho_next, rho_first)
    carried = complex_mul(spread(beta), source)
    direction = (residual[0] + carried[0], residual[1] + carried[1])
    correction = complex_div(complex_mul(beta, rho_next), alpha_first)
    curv_next = (mixed[0] - correction[0], mixed[1] - correction[1])
    alpha_next = complex_div(rho_next, curv_next)
    step_part = complex_mul(spread(alpha_next), direction)
    solution = jnp.stack((first_iterate[0] + step_part[0], first_iterate[1] + step_part[1]), 1)
    terms = moment_terms(solution, angles, radius[0])
    return lax.psum_scatter(terms, "quad", scatter_dimension=3, tiled=True)


def solution(mesh):
    in_specs = (P(None, None, "py", "pz"), P(None, None, "py", "pz"), P(None, "py", "pz"), P(), P())
    out_specs = P(None, None, None, "quad", "py", "pz")
    return jax.shard_map(
        per_device, mesh=mesh, in_specs=in_specs, out_specs=out_specs, check_vma=False
    )
```

profile of v0, /device:TPU:0, one launch (start us, length us, event | category | flops | bytes accessed | tf_op | source)
XLA Modules:
  0.0 492.0 jit_solution(7060185690487794828)
XLA Ops:
  41.0 3.0 copy.95
  45.5 3.0 copy.92
  51.3 4.5 fusion.50
  57.5 3.0 copy.96
  60.7 2.9 copy.94
  63.6 17.7 %fusion.58 = f32[1,2,4,16,16,128]{5,4,3,2,1,0:T(8,128)S(1)} fusion(f32[1,2,4,16,24,4]{5,4,3,2,1,0:T(8,128)} %copy.96, f32[1,2,4,16,24,128]{5,4,3,2,1,0:T(8,128)} %copy.93, f32[1,2,4,16,24,4]{5,4,3,2,1,0:T(8,128)} %copy.94, f32[1,2,4,15,16,128]{5,4,3,2,1,0:T(8,128)} %copy.87, f32[1,2,4,1,16,128]{5,4,3,2,1,0:T(8,128)} %bitcast.76, ...), kind=kLoop, calls=%fused_computation.166 | loop fusion | flops 12845056 | bytes 20676608 | tf_op jit(solution)/shard_map/add | solution.py:46
  82.9 34.7 %all-reduce.1 = (f32[4]{0:T(128)S(1)}, f32[4]{0:T(128)S(1)}, f32[4]{0:T(128)S(1)}, f32[4]{0:T(128)S(1)}) all-reduce(f32[4]{0:T(128)S(1)} %get-tuple-element.10, f32[4]{0:T(128)S(1)} %get-tuple-element.9, f32[4]{0:T(128)S(1)} %get-tuple-element.12, f32[4]{0:T(128)S(1)} %get-tuple-element.11), channel_id=1, replica_groups=mesh['quad'=2,'py'=4,'pz'=4] {'py','pz'}, use_global_device_ids=true, to_apply=%region_7.8 | all-reduce | flops 16 | bytes 128 | tf_op jit(solution)/shard_map/psum | solution.py:102
  124.4 3.5 fusion.31
  133.6 19.1 %copy.121 = f32[4,2,4,16,16,128]{4,3,5,2,1,0:T(8,128)} copy(f32[4,2,4,16,16,128]{5,4,3,2,1,0:T(8,128)} %pad_maximum_fusion.1) | data formatting | bytes 8388608 | tf_op jit(solution)/shard_map/stack | solution.py:114
  155.3 3.4 fusion.29
  158.7 3.2 fusion.27
  161.9 3.4 fusion.25
  165.4 18.9 %copy.122 = f32[4,2,4,16,4,128]{4,3,5,2,1,0:T(8,128)} copy(f32[4,2,4,16,4,128]{5,3,4,2,1,0:T(8,128)} %collective-permute-done.4) | data formatting | bytes 2097152 | tf_op jit(solution)/shard_map/ppermute | solution.py:21
  184.3 18.6 %copy.120 = f32[4,2,4,16,4,128]{4,3,5,2,1,0:T(8,128)} copy(f32[4,2,4,16,4,128]{5,3,4,2,1,0:T(8,128)} %collective-permute-done.5) | data formatting | bytes 2097152 | tf_op jit(solution)/shard_map/ppermute | solution.py:18
  202.9 43.9 %pad_maximum_fusion = f32[4,2,4,16,24,128]{4,3,5,2,1,0:T(8,128)} fusion(f32[4,2,4,16,4,128]{4,3,5,2,1,0:T(8,128)} %copy.122, f32[4,2,4,16,16,128]{4,3,5,2,1,0:T(8,128)} %copy.121, f32[4,2,4,16,4,128]{4,3,5,2,1,0:T(8,128)} %copy.120), kind=kLoop, calls=%fused_computation | loop fusion | flops 3145728 | bytes 12582912 | tf_op jit(solution)/shard_map/concatenate | solution.py:22
  246.8 3.1 fusion.116
  249.9 4.0 collective-permute-start.6
  257.3 5.5 %pad_maximum_fusion.2 = (f32[4,2,4,16,20,128]{5,4,3,2,1,0:T(8,128)}, f32[4,2,4,16,20,128]{5,4,3,2,1,0:T(8,128)}) fusion(f32[4,2,4,16,4,128]{5,4,3,2,1,0:T(4,128)S(1)} %copy.117, f32[4,1,4,16,16,128]{5,4,3,2,1,0:T(8,128)S(1)} %get-tuple-element.48, f32[4,1,4,16,16,128]{5,4,3,2,1,0:T(8,128)S(1)} %copy-done.2, f32[4,2,4,16,4,128]{5,4,3,2,1,0:T(4,128)S(1)} %copy.119), kind=kLoop, calls=%fused_computation.50 | loop fusion | flops 5242880 | bytes 16777216 | tf_op jit(solution)/shard_map/concatenate | solution.py:22
  262.7 22.1 %copy.123 = f32[4,2,4,16,24,128]{5,4,3,2,1,0:T(8,128)} copy(f32[4,2,4,16,24,128]{4,3,5,2,1,0:T(8,128)} %pad_maximum_fusion) | data formatting | bytes 12582912 | tf_op jit(solution)/shard_map/concatenate | solution.py:22
  284.8 6.1 %copy.125 = f32[4,2,4,16,24,4]{5,4,3,2,1,0:T(8,128)} copy(f32[4,2,4,16,24,4]{4,3,5,2,1,0:T(8,128)} %collective-permute-done.7) | data formatting | bytes 393216 | tf_op jit(solution)/shard_map/ppermute | solution.py:18
  291.0 7.0 %collective-permute-done.6 = f32[4,2,4,16,24,4]{4,3,5,2,1,0:T(8,128)} collective-permute-done((f32[4,2,4,16,24,4]{4,3,5,2,1,0:T(8,128)}, f32[4,2,4,16,24,4]{4,3,5,2,1,0:T(8,128)}, u32[]{:S(2)}, u32[]{:S(2)}) %collective-permute-start.6) | collective-permute-done | bytes 196640 | tf_op jit(solution)/shard_map/ppermute | solution.py:21
  298.0 6.0 %copy.124 = f32[4,2,4,16,24,4]{5,4,3,2,1,0:T(8,128)} copy(f32[4,2,4,16,24,4]{4,3,5,2,1,0:T(8,128)} %collective-permute-done.6) | data formatting | bytes 393216 | tf_op jit(solution)/shard_map/ppermute | solution.py:21
  304.0 62.2 %fusion.6 = f32[4,2,4,16,16,128]{5,4,3,2,1,0:T(8,128)} fusion(f32[4,2,4,16,24,4]{5,4,3,2,1,0:T(8,128)} %copy.125, f32[4,2,4,16,24,128]{5,4,3,2,1,0:T(8,128)} %copy.123, f32[4,2,4,16,24,4]{5,4,3,2,1,0:T(8,128)} %copy.124, f32[4,2,4,16,20,128]{5,4,3,2,1,0:T(8,128)} %get-tuple-element.43, f32[4,2,4,16,20,128]{5,4,3,2,1,0:T(8,128)} %get-tuple-element.42, ...), kind=kLoop, calls=%fused_computation.70 | loop fusion | flops 51380224 | bytes 82313216 | tf_op jit(solution)/shard_map/add | solution.py:46
  366.3 5.0 %subtract_reduce_fusion = (f32[4,4]{1,0:T(4,128)S(1)}, f32[4,4]{1,0:T(4,128)S(1)}, f32[4,4]{1,0:T(4,128)S(1)}, f32[4,4]{1,0:T(4,128)S(1)}) fusion(f32[4,2,4,16,16,128]{5,4,3,2,1,0:T(8,128)} %fusion.6, f32[4]{0:T(128)S(1)} %get-tuple-element.88, f32[4]{0:T(128)S(1)} %get-tuple-element.89, f32[4,16,16,128]{3,2,1,0:T(8,128)S(1)} %copy-done.8, ...), kind=kLoop, calls=%fused_computation.129 | loop fusion | flops 20447168 | bytes 6291872 | tf_op jit(solution)/shard_map/reduce_sum | solution.py:63
  371.3 30.6 %all-reduce = (f32[4,4]{1,0:T(4,128)S(1)}, f32[4,4]{1,0:T(4,128)S(1)}, f32[4,4]{1,0:T(4,128)S(1)}, f32[4,4]{1,0:T(4,128)S(1)}) all-reduce(f32[4,4]{1,0:T(4,128)S(1)} %get-tuple-element.8, f32[4,4]{1,0:T(4,128)S(1)} %get-tuple-element.6, f32[4,4]{1,0:T(4,128)S(1)} %get-tuple-element.7, ...), channel_id=1, replica_groups=mesh['quad'=2,'py'=4,'pz'=4] {'py','pz'}, use_global_device_ids=true, to_apply=%region_9.10 | all-reduce | flops 64 | bytes 512 | tf_op jit(solution)/shard_map/psum | solution.py:119
  402.2 2.9 subtract_add_fusion
  405.1 4.4 fusion.34
  409.5 4.4 fusion.36
  413.9 4.6 add_bitcast_fusion
  418.5 4.9 %subtract_bitcast_fusion = f32[4,1,4,16,16,128]{5,0,4,3,2,1:T(4,128)S(1)} fusion(f32[4,4,16,16,128]{4,0,3,2,1:T(4,128)S(1)} %fusion.36, f32[4,4,16,16,128]{4,3,2,1,0:T(8,128)S(1)} %get-tuple-element.46, f32[4]{0:T(128)S(1)} %copy-done.20, f32[4]{0:T(128)S(1)} %copy-done.21, f32[]{:T(128)S(6)} %div.49), kind=kOutput, calls=%fused_computation.123 | convolution fusion | flops 25690144 | bytes 6291492 | tf_op jit(solution)/shard_map/kq,qsxyz->ksxyz/dot_general | solution.py:76
  428.1 53.6 %reduce-scatter.2.cloned.1.call-done = f32[4,2,4,8,16,128]{5,4,2,1,0,3:T(8,128)} async-done(((f32[4,2,4,16,16,128]{5,4,2,1,0,3:T(8,128)}), f32[4,2,4,8,16,128]{5,4,2,1,0,3:T(8,128)}) %reduce-scatter.2.cloned.1.call-update) | async-done | bytes 2097168 | tf_op jit(solution)/shard_map/reduce_scatter | solution.py:131
  481.6 3.2 copy.133
  (128 shorter events, 64.0 us)
Async XLA Ops:
  6.5 475.1 %reduce-scatter.2.cloned.1.call-start = ((), (), s32[]{:S(2)}) async-start(), calls=%async_computation.1 | async-start | bytes 6291456 | tf_op jit(solution)/shard_map/reduce_scatter | solution.py:131
  9.0 28.6 %collective-permute-start = (f32[1,2,4,16,4,128]{5,3,4,2,1,0:T(8,128)}, f32[1,2,4,16,4,128]{5,3,4,2,1,0:T(8,128)}, u32[]{:S(2)}, u32[]{:S(2)}) collective-permute-start(f32[1,2,4,16,4,128]{5,3,4,2,1,0:T(8,128)} %get-tuple-element.83), channel_id=1, source_target_pairs={{4,0},{8,4},{12,8},{0,12},{5,1},{9,5},{13,9},{1,13},{6,2},{10,6},{... | collective-permute-start | bytes 786440 | tf_op jit(solution)/shard_map/ppermute | solution.py:21
  11.4 26.2 %collective-permute-start.1 = (f32[1,2,4,16,4,128]{5,3,4,2,1,0:T(8,128)}, f32[1,2,4,16,4,128]{5,3,4,2,1,0:T(8,128)}, u32[]{:S(2)}, u32[]{:S(2)}) collective-permute-start(f32[1,2,4,16,4,128]{5,3,4,2,1,0:T(8,128)} %get-tuple-element.82), channel_id=1, source_target_pairs={{0,4},{4,8},{8,12},{12,0},{1,5},{5,9},{9,13},{13,1},{2,6},{6,10},{... | collective-permute-start | bytes 786440 | tf_op jit(solution)/shard_map/ppermute | solution.py:18
  20.0 6.3 %copy-start.14 = (f32[1,2,4,14,16,128]{5,3,4,2,1,0:T(8,128)S(1)}, f32[1,2,4,14,16,128]{5,3,4,2,1,0:T(8,128)}, u32[]{:S(2)}) copy-start(f32[1,2,4,14,16,128]{5,3,4,2,1,0:T(8,128)} %get-tuple-element.75) | copy-start | bytes 2752516
  20.0 7.5 %copy-start.19 = (f32[1,2,4,2,16,128]{5,3,4,2,1,0:T(2,128)S(1)}, f32[1,2,4,2,16,128]{5,3,4,2,1,0:T(2,128)}, u32[]{:S(2)}) copy-start(f32[1,2,4,2,16,128]{5,3,4,2,1,0:T(2,128)} %get-tuple-element.77) | copy-start | bytes 393220
  21.1 7.7 %copy-start.13 = (f32[1,2,4,14,16,128]{5,3,4,2,1,0:T(8,128)S(1)}, f32[1,2,4,14,16,128]{5,3,4,2,1,0:T(8,128)}, u32[]{:S(2)}) copy-start(f32[1,2,4,14,16,128]{5,3,4,2,1,0:T(8,128)} %get-tuple-element.74) | copy-start | bytes 2752516
  23.7 6.3 %copy-start.12 = (f32[1,2,4,13,16,128]{5,3,4,2,1,0:T(8,128)S(1)}, f32[1,2,4,13,16,128]{5,3,4,2,1,0:T(8,128)}, u32[]{:S(2)}) copy-start(f32[1,2,4,13,16,128]{5,3,4,2,1,0:T(8,128)} %get-tuple-element.71) | copy-start | bytes 2555908
  27.5 5.1 %copy-start.11 = (f32[1,2,4,13,16,128]{5,3,4,2,1,0:T(8,128)S(1)}, f32[1,2,4,13,16,128]{5,3,4,2,1,0:T(8,128)}, u32[]{:S(2)}) copy-start(f32[1,2,4,13,16,128]{5,3,4,2,1,0:T(8,128)} %get-tuple-element.70) | copy-start | bytes 2555908
  44.0 13.5 %collective-permute-start.3 = (f32[1,2,4,16,24,4]{4,3,5,2,1,0:T(8,128)}, f32[1,2,4,16,24,4]{4,3,5,2,1,0:T(8,128)}, u32[]{:S(2)}, u32[]{:S(2)}) collective-permute-start(f32[1,2,4,16,24,4]{4,3,5,2,1,0:T(8,128)} %copy.95), channel_id=1, source_target_pairs={{0,1},{1,2},{2,3},{3,0},{4,5},{5,6},{6,7},{7,4},{8,9},{9,10},{10,1... | collective-permute-start | bytes 147464 | tf_op jit(solution)/shard_map/ppermute | solution.py:18
  48.5 12.1 %collective-permute-start.2 = (f32[1,2,4,16,24,4]{4,3,5,2,1,0:T(8,128)}, f32[1,2,4,16,24,4]{4,3,5,2,1,0:T(8,128)}, u32[]{:S(2)}, u32[]{:S(2)}) collective-permute-start(f32[1,2,4,16,24,4]{4,3,5,2,1,0:T(8,128)} %copy.92), channel_id=1, source_target_pairs={{1,0},{2,1},{3,2},{0,3},{5,4},{6,5},{7,6},{4,7},{9,8},{10,9},{11,1... | collective-permute-start | bytes 147464 | tf_op jit(solution)/shard_map/ppermute | solution.py:21
  55.8 7.8 %copy-start.3 = (f32[4,16,16,128]{3,2,1,0:T(8,128)S(1)}, f32[4,16,16,128]{3,2,1,0:T(8,128)}, u32[]{:S(2)}) copy-start(f32[4,16,16,128]{3,2,1,0:T(8,128)} %param.6) | copy-start | bytes 1572868
  55.8 7.8 %copy-start.4 = (f32[4,16,16,128]{3,2,1,0:T(8,128)S(1)}, f32[4,16,16,128]{3,2,1,0:T(8,128)}, u32[]{:S(2)}) copy-start(f32[4,16,16,128]{3,2,1,0:T(8,128)} %param.5) | copy-start | bytes 1572868
  55.8 7.8 %copy-start.18 = (f32[16,16,128]{2,1,0:T(8,128)S(1)}, f32[16,16,128]{2,1,0:T(8,128)}, u32[]{:S(2)}) copy-start(f32[16,16,128]{2,1,0:T(8,128)} %param.7) | copy-start | bytes 393220
  57.5 6.1 %copy-start.10 = (f32[1,2,4,16,16,128]{5,3,4,2,1,0:T(8,128)S(1)}, f32[1,2,4,16,16,128]{5,3,4,2,1,0:T(8,128)}, u32[]{:S(2)}) copy-start(f32[1,2,4,16,16,128]{5,3,4,2,1,0:T(8,128)} %get-tuple-element.52) | copy-start | bytes 3145732
  81.3 36.4 %copy-start.5 = (f32[4,16,16,128]{3,2,1,0:T(8,128)S(1)}, f32[4,16,16,128]{3,2,1,0:T(8,128)}, u32[]{:S(2)}) copy-start(f32[4,16,16,128]{3,2,1,0:T(8,128)} %param.5) | copy-start | bytes 1572868
  117.6 11.8 %copy-start.26 = (f32[4]{0:T(128)}, f32[4]{0:T(128)S(1)}, u32[]{:S(2)}) copy-start(f32[4]{0:T(128)S(1)} %get-tuple-element.19) | copy-start | bytes 52
  117.6 11.8 %copy-start.28 = (f32[4]{0:T(128)}, f32[4]{0:T(128)S(1)}, u32[]{:S(2)}) copy-start(f32[4]{0:T(128)S(1)} %get-tuple-element.20) | copy-start | bytes 52
  120.2 12.7 %copy-start = (f32[4,1,4,16,16,128]{5,4,3,2,1,0:T(8,128)}, f32[4,1,4,16,16,128]{5,4,3,2,1,0:T(8,128)S(1)}, u32[]{:S(2)}) copy-start(f32[4,1,4,16,16,128]{5,4,3,2,1,0:T(8,128)S(1)} %get-tuple-element.49) | copy-start | bytes 6291460
  131.1 34.3 %collective-permute-start.4 = (f32[4,2,4,16,4,128]{5,3,4,2,1,0:T(8,128)}, f32[4,2,4,16,4,128]{5,3,4,2,1,0:T(8,128)}, u32[]{:S(2)}, u32[]{:S(2)}) collective-permute-start(f32[4,2,4,16,4,128]{5,3,4,2,1,0:T(8,128)} %copy.144), channel_id=1, source_target_pairs={{4,0},{8,4},{12,8},{0,12},{5,1},{9,5},{13,9},{1,13},{6,2},{10,6},{... | collective-permute-start | bytes 3145736 | tf_op jit(solution)/shard_map/ppermute | solution.py:21
  132.2 52.1 %collective-permute-start.5 = (f32[4,2,4,16,4,128]{5,3,4,2,1,0:T(8,128)}, f32[4,2,4,16,4,128]{5,3,4,2,1,0:T(8,128)}, u32[]{:S(2)}, u32[]{:S(2)}) collective-permute-start(f32[4,2,4,16,4,128]{5,3,4,2,1,0:T(8,128)} %copy.145), channel_id=1, source_target_pairs={{0,4},{4,8},{8,12},{12,0},{1,5},{5,9},{9,13},{13,1},{2,6},{6,10},{... | collective-permute-start | bytes 3145736 | tf_op jit(solution)/shard_map/ppermute | solution.py:18
  249.9 7.3 %copy-start.2 = (f32[4,1,4,16,16,128]{5,4,3,2,1,0:T(8,128)S(1)}, f32[4,1,4,16,16,128]{5,4,3,2,1,0:T(8,128)}, u32[]{:S(2)}) copy-start(f32[4,1,4,16,16,128]{5,4,3,2,1,0:T(8,128)} %copy-done) | copy-start | bytes 6291460
  249.9 34.9 %collective-permute-start.7 = (f32[4,2,4,16,24,4]{4,3,5,2,1,0:T(8,128)}, f32[4,2,4,16,24,4]{4,3,5,2,1,0:T(8,128)}, u32[]{:S(2)}, u32[]{:S(2)}) collective-permute-start(f32[4,2,4,16,24,4]{4,3,5,2,1,0:T(8,128)} %get-tuple-element.25), channel_id=1, source_target_pairs={{0,1},{1,2},{2,3},{3,0},{4,5},{5,6},{6,7},{7,4},{8,9},{9,10},{10,1... | collective-permute-start | bytes 589832 | tf_op jit(solution)/shard_map/ppermute | solution.py:18
  249.9 48.1 %collective-permute-start.6 = (f32[4,2,4,16,24,4]{4,3,5,2,1,0:T(8,128)}, f32[4,2,4,16,24,4]{4,3,5,2,1,0:T(8,128)}, u32[]{:S(2)}, u32[]{:S(2)}) collective-permute-start(f32[4,2,4,16,24,4]{4,3,5,2,1,0:T(8,128)} %get-tuple-element.24), channel_id=1, source_target_pairs={{1,0},{2,1},{3,2},{0,3},{5,4},{6,5},{7,6},{4,7},{9,8},{10,9},{11,1... | collective-permute-start | bytes 589832 | tf_op jit(solution)/shard_map/ppermute | solution.py:21
  304.0 62.2 %copy-start.6 = (f32[4,16,16,128]{3,2,1,0:T(8,128)S(1)}, f32[4,16,16,128]{3,2,1,0:T(8,128)}, u32[]{:S(2)}) copy-start(f32[4,16,16,128]{3,2,1,0:T(8,128)} %get-tuple-element.60) | copy-start | bytes 1572868
  304.0 62.2 %copy-start.8 = (f32[4,16,16,128]{3,2,1,0:T(8,128)S(1)}, f32[4,16,16,128]{3,2,1,0:T(8,128)}, u32[]{:S(2)}) copy-start(f32[4,16,16,128]{3,2,1,0:T(8,128)} %get-tuple-element.61) | copy-start | bytes 1572868
  366.3 35.7 %copy-start.23 = (f32[4]{0:T(128)S(1)}, f32[4]{0:T(128)}, u32[]{:S(2)}) copy-start(f32[4]{0:T(128)} %copy-done.22) | copy-start | bytes 52
  366.3 35.7 %copy-start.25 = (f32[4]{0:T(128)S(1)}, f32[4]{0:T(128)}, u32[]{:S(2)}) copy-start(f32[4]{0:T(128)} %copy-done.24) | copy-start | bytes 52
  366.3 35.7 %copy-start.27 = (f32[4]{0:T(128)S(1)}, f32[4]{0:T(128)}, u32[]{:S(2)}) copy-start(f32[4]{0:T(128)} %copy-done.26) | copy-start | bytes 52
  366.3 35.7 %copy-start.29 = (f32[4]{0:T(128)S(1)}, f32[4]{0:T(128)}, u32[]{:S(2)}) copy-start(f32[4]{0:T(128)} %copy-done.28) | copy-start | bytes 52
  366.3 35.7 %copy-start.30 = (f32[4]{0:T(128)S(1)}, f32[4]{0:T(128)}, u32[]{:S(2)}) copy-start(f32[4]{0:T(128)} %multiply_add_fusion.4) | copy-start | bytes 52
  366.3 35.8 %copy-start.7 = (f32[4,16,16,128]{3,2,1,0:T(8,128)S(1)}, f32[4,16,16,128]{3,2,1,0:T(8,128)}, u32[]{:S(2)}) copy-start(f32[4,16,16,128]{3,2,1,0:T(8,128)} %get-tuple-element.60) | copy-start | bytes 1572868
  366.3 35.8 %copy-start.9 = (f32[4,16,16,128]{3,2,1,0:T(8,128)S(1)}, f32[4,16,16,128]{3,2,1,0:T(8,128)}, u32[]{:S(2)}) copy-start(f32[4,16,16,128]{3,2,1,0:T(8,128)} %get-tuple-element.61) | copy-start | bytes 1572868
  (8 other events, 28.2 us)
Sparse Core Ops, SparseCore 0:
  428.2 53.3 reduce-scatter.1
where the time goes:
time: 499 us; the launch traced here: 492 us
  other arithmetic  173 us (35%)
  local copies, waits for them, and re-layouts  147 us (29%)
  blocking collectives  65.3 us (13%)
  waiting for transfers between devices  60.8 us (12%)
  matrix products  18.3 us (4%)
  between operations  15.5 us (3%)
  starting transfers between devices  11.4 us (2%)
    add x2, other arithmetic, apply_operator(): return -0.5 * laplace + potential * field  79.9 us
    concatenate x4, other arithmetic, padded_2(): block = jnp.concatenate([low, block, high], axis=dim)  55 us
    reduce_scatter x1, waiting for transfers between devices, per_device(): return lax.psum_scatter(terms, 'quad', scatter_dimension=3, tiled=True)  53.6 us
    psum x1, blocking collectives, per_device(): lax.psum((rho_local[0], rho_local[1], curv_local[0], curv_local[1]), ('py...  34.7 us
    psum x1, blocking collectives, per_device(): lax.psum((rho_part[0], rho_part[1], mixed_part[0], mixed_part[1]), ('py',...  30.6 us
    ppermute x4, local copies, waits for them, and re-layouts, padded_2(): lax.ppermute(lax.slice_in_dim(block, 0, width, axis=dim), axis, backward)  29.5 us
    ppermute x4, local copies, waits for them, and re-layouts, padded_2(): lax.ppermute(lax.slice_in_dim(block, block.shape[dim] - width, None, axis...  29.4 us
    concatenate x2, local copies, waits for them, and re-layouts, padded_2(): block = jnp.concatenate([low, block, high], axis=dim)  23.7 us
  transfers between devices with their start and end apart: 9, of which 3 were waited for; matrix products, arithmetic and copies ran while one was open for 26% of the time, Pallas kernels for 0%

commit v1 on v0

--- a/solution.py
+++ b/solution.py
@@ -99,7 +99,9 @@
     hsource = (applied[0], applied[1])
     rho_local = local_bilinear(source, source)
     curv_local = local_bilinear(source, hsource)
-    totals = lax.psum((rho_local[0], rho_local[1], curv_local[0], curv_local[1]), ("py", "pz"))
+    totals = lax.psum(
+        lax.psum((rho_local[0], rho_local[1], curv_local[0], curv_local[1]), "py"), "pz"
+    )
     rho_first = (totals[0], totals[1])
     curv_first = (totals[2], totals[3])
     scaled = complex_mul(shift_pair, rho_first)

time: 499 us -> 485 us (0.972)
  blocking collectives: 65.3 us -> 52 us
    psum x1 -> x2, blocking collectives: 34.7 us -> 19.6 us  [the longest x1 12.9 us: per_device(): lax.psum(lax.psum((rho_local[0], rho_local[1], curv_local[0], curv_local[...]
where the time goes in v1:
time: 485 us; the launch traced here: 478 us
  other arithmetic  174 us (36%)
  local copies, waits for them, and re-layouts  147 us (30%)
  waiting for transfers between devices  59.6 us (12%)
  blocking collectives  52 us (11%)
  matrix products  18.3 us (4%)
  between operations  15.5 us (3%)
  starting transfers between devices  11.4 us (2%)
    add x2, other arithmetic, apply_operator(): return -0.5 * laplace + potential * field  80.9 us
    concatenate x4, other arithmetic, padded_2(): block = jnp.concatenate([low, block, high], axis=dim)  54.9 us
    reduce_scatter x1, waiting for transfers between devices, per_device(): return lax.psum_scatter(terms, 'quad', scatter_dimension=3, tiled=True)  52.3 us
    psum x1, blocking collectives, per_device(): lax.psum((rho_part[0], rho_part[1], mixed_part[0], mixed_part[1]), ('py',...  32.4 us
    ppermute x4, local copies, waits for them, and re-layouts, padded_2(): lax.ppermute(lax.slice_in_dim(block, 0, width, axis=dim), axis, backward)  29.5 us
    ppermute x4, local copies, waits for them, and re-layouts, padded_2(): lax.ppermute(lax.slice_in_dim(block, block.shape[dim] - width, None, axis...  29.4 us
    concatenate x2, local copies, waits for them, and re-layouts, padded_2(): block = jnp.concatenate([low, block, high], axis=dim)  23.7 us
    slice x22, local copies, waits for them, and re-layouts, apply_operator(): beside_all = jnp.roll(field, offset, 3) + jnp.roll(field, -offset, 3)  23.7 us
  transfers between devices with their start and end apart: 9, of which 3 were waited for; matrix products, arithmetic and copies ran while one was open for 26% of the time, Pallas kernels for 0%

profile of v1, /device:TPU:0, one launch (start us, length us, event | category | flops | bytes accessed | tf_op | source)
XLA Modules:
  0.0 478.3 jit_solution(2086190551319542798)
XLA Ops:
  41.0 3.0 copy.95
  45.5 3.0 copy.92
  51.3 4.5 fusion.50
  57.5 3.0 copy.96
  60.6 2.9 copy.94
  63.6 17.9 %fusion.58 = f32[1,2,4,16,16,128]{5,4,3,2,1,0:T(8,128)S(1)} fusion(f32[1,2,4,16,24,4]{5,4,3,2,1,0:T(8,128)} %copy.96, f32[1,2,4,16,24,128]{5,4,3,2,1,0:T(8,128)} %copy.93, f32[1,2,4,16,24,4]{5,4,3,2,1,0:T(8,128)} %copy.94, f32[1,2,4,15,16,128]{5,4,3,2,1,0:T(8,128)} %copy.87, f32[1,2,4,1,16,128]{5,4,3,2,1,0:T(8,128)} %bitcast.76, ...), kind=kLoop, calls=%fused_computation.166 | loop fusion | flops 12845056 | bytes 20676608 | tf_op jit(solution)/shard_map/add | solution.py:46
  83.0 6.7 %all-reduce.2 = (f32[4]{0:T(128)S(1)}, f32[4]{0:T(128)S(1)}, f32[4]{0:T(128)S(1)}, f32[4]{0:T(128)S(1)}) all-reduce(f32[4]{0:T(128)S(1)} %get-tuple-element.10, f32[4]{0:T(128)S(1)} %get-tuple-element.9, f32[4]{0:T(128)S(1)} %get-tuple-element.12, f32[4]{0:T(128)S(1)} %get-tuple-element.11), channel_id=1, replica_groups=mesh['quad'=2,'py'=4,'pz'=4] {'py'}, use_global_device_ids=true, to_apply=%region_10.11 | all-reduce | flops 16 | bytes 128 | tf_op jit(solution)/shard_map/psum | solution.py:103
  89.7 12.9 %all-reduce.1 = (f32[4]{0:T(128)S(1)}, f32[4]{0:T(128)S(1)}, f32[4]{0:T(128)S(1)}, f32[4]{0:T(128)S(1)}) all-reduce(f32[4]{0:T(128)S(1)} %get-tuple-element.21, f32[4]{0:T(128)S(1)} %get-tuple-element.22, f32[4]{0:T(128)S(1)} %get-tuple-element.23, f32[4]{0:T(128)S(1)} %get-tuple-element.24), channel_id=1, replica_groups=mesh['quad'=2,'py'=4,'pz'=4] {'pz'}, use_global_device_ids=true, to_apply=%region_11.12 | all-reduce | flops 16 | bytes 128 | tf_op jit(solution)/shard_map/psum | solution.py:102
  109.4 3.5 fusion.31
  118.6 19.1 %copy.121 = f32[4,2,4,16,16,128]{4,3,5,2,1,0:T(8,128)} copy(f32[4,2,4,16,16,128]{5,4,3,2,1,0:T(8,128)} %pad_maximum_fusion.1) | data formatting | bytes 8388608 | tf_op jit(solution)/shard_map/stack | solution.py:116
  140.3 3.4 fusion.29
  143.7 3.2 fusion.27
  147.0 3.4 fusion.25
  150.4 18.9 %copy.122 = f32[4,2,4,16,4,128]{4,3,5,2,1,0:T(8,128)} copy(f32[4,2,4,16,4,128]{5,3,4,2,1,0:T(8,128)} %collective-permute-done.4) | data formatting | bytes 2097152 | tf_op jit(solution)/shard_map/ppermute | solution.py:21
  169.3 18.6 %copy.120 = f32[4,2,4,16,4,128]{4,3,5,2,1,0:T(8,128)} copy(f32[4,2,4,16,4,128]{5,3,4,2,1,0:T(8,128)} %collective-permute-done.5) | data formatting | bytes 2097152 | tf_op jit(solution)/shard_map/ppermute | solution.py:18
  187.9 43.9 %pad_maximum_fusion = f32[4,2,4,16,24,128]{4,3,5,2,1,0:T(8,128)} fusion(f32[4,2,4,16,4,128]{4,3,5,2,1,0:T(8,128)} %copy.122, f32[4,2,4,16,16,128]{4,3,5,2,1,0:T(8,128)} %copy.121, f32[4,2,4,16,4,128]{4,3,5,2,1,0:T(8,128)} %copy.120), kind=kLoop, calls=%fused_computation | loop fusion | flops 3145728 | bytes 12582912 | tf_op jit(solution)/shard_map/concatenate | solution.py:22
  231.7 3.1 fusion.116
  234.9 4.0 collective-permute-start.6
  242.2 5.5 %pad_maximum_fusion.2 = (f32[4,2,4,16,20,128]{5,4,3,2,1,0:T(8,128)}, f32[4,2,4,16,20,128]{5,4,3,2,1,0:T(8,128)}) fusion(f32[4,2,4,16,4,128]{5,4,3,2,1,0:T(4,128)S(1)} %copy.117, f32[4,1,4,16,16,128]{5,4,3,2,1,0:T(8,128)S(1)} %get-tuple-element.52, f32[4,1,4,16,16,128]{5,4,3,2,1,0:T(8,128)S(1)} %copy-done.2, f32[4,2,4,16,4,128]{5,4,3,2,1,0:T(4,128)S(1)} %copy.119), kind=kLoop, calls=%fused_computation.50 | loop fusion | flops 5242880 | bytes 16777216 | tf_op jit(solution)/shard_map/concatenate | solution.py:22
  247.7 22.1 %copy.123 = f32[4,2,4,16,24,128]{5,4,3,2,1,0:T(8,128)} copy(f32[4,2,4,16,24,128]{4,3,5,2,1,0:T(8,128)} %pad_maximum_fusion) | data formatting | bytes 12582912 | tf_op jit(solution)/shard_map/concatenate | solution.py:22
  269.7 6.1 %copy.125 = f32[4,2,4,16,24,4]{5,4,3,2,1,0:T(8,128)} copy(f32[4,2,4,16,24,4]{4,3,5,2,1,0:T(8,128)} %collective-permute-done.7) | data formatting | bytes 393216 | tf_op jit(solution)/shard_map/ppermute | solution.py:18
  275.8 7.1 %collective-permute-done.6 = f32[4,2,4,16,24,4]{4,3,5,2,1,0:T(8,128)} collective-permute-done((f32[4,2,4,16,24,4]{4,3,5,2,1,0:T(8,128)}, f32[4,2,4,16,24,4]{4,3,5,2,1,0:T(8,128)}, u32[]{:S(2)}, u32[]{:S(2)}) %collective-permute-start.6) | collective-permute-done | bytes 196640 | tf_op jit(solution)/shard_map/ppermute | solution.py:21
  282.9 6.0 %copy.124 = f32[4,2,4,16,24,4]{5,4,3,2,1,0:T(8,128)} copy(f32[4,2,4,16,24,4]{4,3,5,2,1,0:T(8,128)} %collective-permute-done.6) | data formatting | bytes 393216 | tf_op jit(solution)/shard_map/ppermute | solution.py:21
  289.0 63.1 %fusion.6 = f32[4,2,4,16,16,128]{5,4,3,2,1,0:T(8,128)} fusion(f32[4,2,4,16,24,4]{5,4,3,2,1,0:T(8,128)} %copy.125, f32[4,2,4,16,24,128]{5,4,3,2,1,0:T(8,128)} %copy.123, f32[4,2,4,16,24,4]{5,4,3,2,1,0:T(8,128)} %copy.124, f32[4,2,4,16,20,128]{5,4,3,2,1,0:T(8,128)} %get-tuple-element.47, f32[4,2,4,16,20,128]{5,4,3,2,1,0:T(8,128)} %get-tuple-element.46, ...), kind=kLoop, calls=%fused_computation.70 | loop fusion | flops 51380224 | bytes 82313216 | tf_op jit(solution)/shard_map/add | solution.py:46
  352.1 5.0 %subtract_reduce_fusion = (f32[4,4]{1,0:T(4,128)S(1)}, f32[4,4]{1,0:T(4,128)S(1)}, f32[4,4]{1,0:T(4,128)S(1)}, f32[4,4]{1,0:T(4,128)S(1)}) fusion(f32[4,2,4,16,16,128]{5,4,3,2,1,0:T(8,128)} %fusion.6, f32[4]{0:T(128)S(1)} %get-tuple-element.92, f32[4]{0:T(128)S(1)} %get-tuple-element.93, f32[4,16,16,128]{3,2,1,0:T(8,128)S(1)} %copy-done.8, ...), kind=kLoop, calls=%fused_computation.129 | loop fusion | flops 20447168 | bytes 6291872 | tf_op jit(solution)/shard_map/reduce_sum | solution.py:63
  357.1 32.4 %all-reduce = (f32[4,4]{1,0:T(4,128)S(1)}, f32[4,4]{1,0:T(4,128)S(1)}, f32[4,4]{1,0:T(4,128)S(1)}, f32[4,4]{1,0:T(4,128)S(1)}) all-reduce(f32[4,4]{1,0:T(4,128)S(1)} %get-tuple-element.8, f32[4,4]{1,0:T(4,128)S(1)} %get-tuple-element.6, f32[4,4]{1,0:T(4,128)S(1)} %get-tuple-element.7, ...), channel_id=1, replica_groups=mesh['quad'=2,'py'=4,'pz'=4] {'py','pz'}, use_global_device_ids=true, to_apply=%region_13.14 | all-reduce | flops 64 | bytes 512 | tf_op jit(solution)/shard_map/psum | solution.py:121
  392.6 4.4 fusion.34
  397.0 4.4 fusion.36
  401.4 4.6 add_bitcast_fusion
  406.0 4.9 %subtract_bitcast_fusion = f32[4,1,4,16,16,128]{5,0,4,3,2,1:T(4,128)S(1)} fusion(f32[4,4,16,16,128]{4,0,3,2,1:T(4,128)S(1)} %fusion.36, f32[4,4,16,16,128]{4,3,2,1,0:T(8,128)S(1)} %get-tuple-element.50, f32[4]{0:T(128)S(1)} %copy-done.20, f32[4]{0:T(128)S(1)} %copy-done.21, f32[]{:T(128)S(6)} %div.49), kind=kOutput, calls=%fused_computation.123 | convolution fusion | flops 25690144 | bytes 6291492 | tf_op jit(solution)/shard_map/kq,qsxyz->ksxyz/dot_general | solution.py:76
  415.6 52.3 %reduce-scatter.2.cloned.1.call-done = f32[4,2,4,8,16,128]{5,4,2,1,0,3:T(8,128)} async-done(((f32[4,2,4,16,16,128]{5,4,2,1,0,3:T(8,128)}), f32[4,2,4,8,16,128]{5,4,2,1,0,3:T(8,128)}) %reduce-scatter.2.cloned.1.call-update) | async-done | bytes 2097168 | tf_op jit(solution)/shard_map/reduce_scatter | solution.py:133
  467.9 3.2 copy.133
  (129 shorter events, 66.9 us)
Async XLA Ops:
  6.5 461.4 %reduce-scatter.2.cloned.1.call-start = ((), (), s32[]{:S(2)}) async-start(), calls=%async_computation.1 | async-start | bytes 6291456 | tf_op jit(solution)/shard_map/reduce_scatter | solution.py:133
  9.0 28.6 %collective-permute-start = (f32[1,2,4,16,4,128]{5,3,4,2,1,0:T(8,128)}, f32[1,2,4,16,4,128]{5,3,4,2,1,0:T(8,128)}, u32[]{:S(2)}, u32[]{:S(2)}) collective-permute-start(f32[1,2,4,16,4,128]{5,3,4,2,1,0:T(8,128)} %get-tuple-element.87), channel_id=1, source_target_pairs={{4,0},{8,4},{12,8},{0,12},{5,1},{9,5},{13,9},{1,13},{6,2},{10,6},{... | collective-permute-start | bytes 786440 | tf_op jit(solution)/shard_map/ppermute | solution.py:21
  11.4 26.2 %collective-permute-start.1 = (f32[1,2,4,16,4,128]{5,3,4,2,1,0:T(8,128)}, f32[1,2,4,16,4,128]{5,3,4,2,1,0:T(8,128)}, u32[]{:S(2)}, u32[]{:S(2)}) collective-permute-start(f32[1,2,4,16,4,128]{5,3,4,2,1,0:T(8,128)} %get-tuple-element.86), channel_id=1, source_target_pairs={{0,4},{4,8},{8,12},{12,0},{1,5},{5,9},{9,13},{13,1},{2,6},{6,10},{... | collective-permute-start | bytes 786440 | tf_op jit(solution)/shard_map/ppermute | solution.py:18
  20.0 6.3 %copy-start.14 = (f32[1,2,4,14,16,128]{5,3,4,2,1,0:T(8,128)S(1)}, f32[1,2,4,14,16,128]{5,3,4,2,1,0:T(8,128)}, u32[]{:S(2)}) copy-start(f32[1,2,4,14,16,128]{5,3,4,2,1,0:T(8,128)} %get-tuple-element.79) | copy-start | bytes 2752516
  20.0 7.5 %copy-start.19 = (f32[1,2,4,2,16,128]{5,3,4,2,1,0:T(2,128)S(1)}, f32[1,2,4,2,16,128]{5,3,4,2,1,0:T(2,128)}, u32[]{:S(2)}) copy-start(f32[1,2,4,2,16,128]{5,3,4,2,1,0:T(2,128)} %get-tuple-element.81) | copy-start | bytes 393220
  21.1 7.7 %copy-start.13 = (f32[1,2,4,14,16,128]{5,3,4,2,1,0:T(8,128)S(1)}, f32[1,2,4,14,16,128]{5,3,4,2,1,0:T(8,128)}, u32[]{:S(2)}) copy-start(f32[1,2,4,14,16,128]{5,3,4,2,1,0:T(8,128)} %get-tuple-element.78) | copy-start | bytes 2752516
  23.7 6.4 %copy-start.12 = (f32[1,2,4,13,16,128]{5,3,4,2,1,0:T(8,128)S(1)}, f32[1,2,4,13,16,128]{5,3,4,2,1,0:T(8,128)}, u32[]{:S(2)}) copy-start(f32[1,2,4,13,16,128]{5,3,4,2,1,0:T(8,128)} %get-tuple-element.75) | copy-start | bytes 2555908
  27.5 5.1 %copy-start.11 = (f32[1,2,4,13,16,128]{5,3,4,2,1,0:T(8,128)S(1)}, f32[1,2,4,13,16,128]{5,3,4,2,1,0:T(8,128)}, u32[]{:S(2)}) copy-start(f32[1,2,4,13,16,128]{5,3,4,2,1,0:T(8,128)} %get-tuple-element.74) | copy-start | bytes 2555908
  44.0 13.5 %collective-permute-start.3 = (f32[1,2,4,16,24,4]{4,3,5,2,1,0:T(8,128)}, f32[1,2,4,16,24,4]{4,3,5,2,1,0:T(8,128)}, u32[]{:S(2)}, u32[]{:S(2)}) collective-permute-start(f32[1,2,4,16,24,4]{4,3,5,2,1,0:T(8,128)} %copy.95), channel_id=1, source_target_pairs={{0,1},{1,2},{2,3},{3,0},{4,5},{5,6},{6,7},{7,4},{8,9},{9,10},{10,1... | collective-permute-start | bytes 147464 | tf_op jit(solution)/shard_map/ppermute | solution.py:18
  48.5 12.1 %collective-permute-start.2 = (f32[1,2,4,16,24,4]{4,3,5,2,1,0:T(8,128)}, f32[1,2,4,16,24,4]{4,3,5,2,1,0:T(8,128)}, u32[]{:S(2)}, u32[]{:S(2)}) collective-permute-start(f32[1,2,4,16,24,4]{4,3,5,2,1,0:T(8,128)} %copy.92), channel_id=1, source_target_pairs={{1,0},{2,1},{3,2},{0,3},{5,4},{6,5},{7,6},{4,7},{9,8},{10,9},{11,1... | collective-permute-start | bytes 147464 | tf_op jit(solution)/shard_map/ppermute | solution.py:21
  55.8 7.8 %copy-start.3 = (f32[4,16,16,128]{3,2,1,0:T(8,128)S(1)}, f32[4,16,16,128]{3,2,1,0:T(8,128)}, u32[]{:S(2)}) copy-start(f32[4,16,16,128]{3,2,1,0:T(8,128)} %param.6) | copy-start | bytes 1572868
  55.8 7.8 %copy-start.4 = (f32[4,16,16,128]{3,2,1,0:T(8,128)S(1)}, f32[4,16,16,128]{3,2,1,0:T(8,128)}, u32[]{:S(2)}) copy-start(f32[4,16,16,128]{3,2,1,0:T(8,128)} %param.5) | copy-start | bytes 1572868
  55.8 7.8 %copy-start.18 = (f32[16,16,128]{2,1,0:T(8,128)S(1)}, f32[16,16,128]{2,1,0:T(8,128)}, u32[]{:S(2)}) copy-start(f32[16,16,128]{2,1,0:T(8,128)} %param.7) | copy-start | bytes 393220
  57.5 6.1 %copy-start.10 = (f32[1,2,4,16,16,128]{5,3,4,2,1,0:T(8,128)S(1)}, f32[1,2,4,16,16,128]{5,3,4,2,1,0:T(8,128)}, u32[]{:S(2)}) copy-start(f32[1,2,4,16,16,128]{5,3,4,2,1,0:T(8,128)} %get-tuple-element.56) | copy-start | bytes 3145732
  81.4 21.3 %copy-start.5 = (f32[4,16,16,128]{3,2,1,0:T(8,128)S(1)}, f32[4,16,16,128]{3,2,1,0:T(8,128)}, u32[]{:S(2)}) copy-start(f32[4,16,16,128]{3,2,1,0:T(8,128)} %param.5) | copy-start | bytes 1572868
  102.6 11.9 %copy-start.26 = (f32[4]{0:T(128)}, f32[4]{0:T(128)S(1)}, u32[]{:S(2)}) copy-start(f32[4]{0:T(128)S(1)} %get-tuple-element.19) | copy-start | bytes 52
  102.6 11.8 %copy-start.28 = (f32[4]{0:T(128)}, f32[4]{0:T(128)S(1)}, u32[]{:S(2)}) copy-start(f32[4]{0:T(128)S(1)} %get-tuple-element.20) | copy-start | bytes 52
  105.2 12.7 %copy-start = (f32[4,1,4,16,16,128]{5,4,3,2,1,0:T(8,128)}, f32[4,1,4,16,16,128]{5,4,3,2,1,0:T(8,128)S(1)}, u32[]{:S(2)}) copy-start(f32[4,1,4,16,16,128]{5,4,3,2,1,0:T(8,128)S(1)} %get-tuple-element.53) | copy-start | bytes 6291460
  116.1 34.3 %collective-permute-start.4 = (f32[4,2,4,16,4,128]{5,3,4,2,1,0:T(8,128)}, f32[4,2,4,16,4,128]{5,3,4,2,1,0:T(8,128)}, u32[]{:S(2)}, u32[]{:S(2)}) collective-permute-start(f32[4,2,4,16,4,128]{5,3,4,2,1,0:T(8,128)} %copy.144), channel_id=1, source_target_pairs={{4,0},{8,4},{12,8},{0,12},{5,1},{9,5},{13,9},{1,13},{6,2},{10,6},{... | collective-permute-start | bytes 3145736 | tf_op jit(solution)/shard_map/ppermute | solution.py:21
  117.2 52.1 %collective-permute-start.5 = (f32[4,2,4,16,4,128]{5,3,4,2,1,0:T(8,128)}, f32[4,2,4,16,4,128]{5,3,4,2,1,0:T(8,128)}, u32[]{:S(2)}, u32[]{:S(2)}) collective-permute-start(f32[4,2,4,16,4,128]{5,3,4,2,1,0:T(8,128)} %copy.145), channel_id=1, source_target_pairs={{0,4},{4,8},{8,12},{12,0},{1,5},{5,9},{9,13},{13,1},{2,6},{6,10},{... | collective-permute-start | bytes 3145736 | tf_op jit(solution)/shard_map/ppermute | solution.py:18
  234.9 7.3 %copy-start.2 = (f32[4,1,4,16,16,128]{5,4,3,2,1,0:T(8,128)S(1)}, f32[4,1,4,16,16,128]{5,4,3,2,1,0:T(8,128)}, u32[]{:S(2)}) copy-start(f32[4,1,4,16,16,128]{5,4,3,2,1,0:T(8,128)} %copy-done) | copy-start | bytes 6291460
  234.9 34.9 %collective-permute-start.7 = (f32[4,2,4,16,24,4]{4,3,5,2,1,0:T(8,128)}, f32[4,2,4,16,24,4]{4,3,5,2,1,0:T(8,128)}, u32[]{:S(2)}, u32[]{:S(2)}) collective-permute-start(f32[4,2,4,16,24,4]{4,3,5,2,1,0:T(8,128)} %get-tuple-element.29), channel_id=1, source_target_pairs={{0,1},{1,2},{2,3},{3,0},{4,5},{5,6},{6,7},{7,4},{8,9},{9,10},{10,1... | collective-permute-start | bytes 589832 | tf_op jit(solution)/shard_map/ppermute | solution.py:18
  234.9 48.1 %collective-permute-start.6 = (f32[4,2,4,16,24,4]{4,3,5,2,1,0:T(8,128)}, f32[4,2,4,16,24,4]{4,3,5,2,1,0:T(8,128)}, u32[]{:S(2)}, u32[]{:S(2)}) collective-permute-start(f32[4,2,4,16,24,4]{4,3,5,2,1,0:T(8,128)} %get-tuple-element.28), channel_id=1, source_target_pairs={{1,0},{2,1},{3,2},{0,3},{5,4},{6,5},{7,6},{4,7},{9,8},{10,9},{11,1... | collective-permute-start | bytes 589832 | tf_op jit(solution)/shard_map/ppermute | solution.py:21
  289.0 63.1 %copy-start.6 = (f32[4,16,16,128]{3,2,1,0:T(8,128)S(1)}, f32[4,16,16,128]{3,2,1,0:T(8,128)}, u32[]{:S(2)}) copy-start(f32[4,16,16,128]{3,2,1,0:T(8,128)} %get-tuple-element.64) | copy-start | bytes 1572868
  289.0 63.1 %copy-start.8 = (f32[4,16,16,128]{3,2,1,0:T(8,128)S(1)}, f32[4,16,16,128]{3,2,1,0:T(8,128)}, u32[]{:S(2)}) copy-start(f32[4,16,16,128]{3,2,1,0:T(8,128)} %get-tuple-element.65) | copy-start | bytes 1572868
  352.1 37.4 %copy-start.23 = (f32[4]{0:T(128)S(1)}, f32[4]{0:T(128)}, u32[]{:S(2)}) copy-start(f32[4]{0:T(128)} %copy-done.22) | copy-start | bytes 52
  352.1 37.4 %copy-start.25 = (f32[4]{0:T(128)S(1)}, f32[4]{0:T(128)}, u32[]{:S(2)}) copy-start(f32[4]{0:T(128)} %copy-done.24) | copy-start | bytes 52
  352.1 37.4 %copy-start.27 = (f32[4]{0:T(128)S(1)}, f32[4]{0:T(128)}, u32[]{:S(2)}) copy-start(f32[4]{0:T(128)} %copy-done.26) | copy-start | bytes 52
  352.1 37.4 %copy-start.29 = (f32[4]{0:T(128)S(1)}, f32[4]{0:T(128)}, u32[]{:S(2)}) copy-start(f32[4]{0:T(128)} %copy-done.28) | copy-start | bytes 52
  352.1 37.4 %copy-start.30 = (f32[4]{0:T(128)S(1)}, f32[4]{0:T(128)}, u32[]{:S(2)}) copy-start(f32[4]{0:T(128)} %multiply_add_fusion.4) | copy-start | bytes 52
  352.1 37.6 %copy-start.7 = (f32[4,16,16,128]{3,2,1,0:T(8,128)S(1)}, f32[4,16,16,128]{3,2,1,0:T(8,128)}, u32[]{:S(2)}) copy-start(f32[4,16,16,128]{3,2,1,0:T(8,128)} %get-tuple-element.64) | copy-start | bytes 1572868
  352.1 37.6 %copy-start.9 = (f32[4,16,16,128]{3,2,1,0:T(8,128)S(1)}, f32[4,16,16,128]{3,2,1,0:T(8,128)}, u32[]{:S(2)}) copy-start(f32[4,16,16,128]{3,2,1,0:T(8,128)} %get-tuple-element.65) | copy-start | bytes 1572868
  (8 other events, 28.2 us)
Sparse Core Ops, SparseCore 0:
  415.8 52.1 reduce-scatter.1
